TPU v7x, 32 devices: a whole 2x2x4 slice. The times are simulated.
32 devices in a mesh: shard: 4 (over y, x), context: 8 (over z, core).
Axes of the slice: x: 2, y: 2, z: 4, core: 2. Of those that a mesh axis runs over, the one named last changes fastest.
Arguments:
- tokens: bfloat16 [4096, 1536], P(('shard', 'context')), may hold values from -6 to 6
- segments: int32 [4096], P(('shard', 'context')), may hold values from 0 to 3, as said below
- positions: int32 [4096], P(('shard', 'context')), may hold values from 0 to 1022, as said below
- attn_gain: float32 [1536], replicated, may hold values from 0.5 to 1.5
- w_qkv: bfloat16 [1536, 2048], P('shard'), may hold values from -0.15625 to 0.15625
- b_qkv: float32 [2048], replicated, may hold values from -3 to 3
- w_out: bfloat16 [1536, 1536], P('shard'), may hold values from -0.625 to 0.625
- ffn_gain: float32 [1536], replicated, may hold values from 0.5 to 1.5
- w_gate_up: bfloat16 [1536, 2, 8960], P('shard', None, 'context'), may hold values from -0.15625 to 0.15625
- w_down: bfloat16 [8960, 1536], P('context', 'shard'), may hold values from -0.1875 to 0.1875
- cotangent: bfloat16 [4096, 1536], P(('shard', 'context')), may hold values from -6 to 6
Outputs:
- output: float32 [4096, 1536], P(('shard', 'context'))
- grad_tokens: float32 [4096, 1536], P(('shard', 'context'))
- grad_attn_gain: float32 [1536], P(('shard', 'context'))
- grad_w_qkv: float32 [1536, 2048], P(('shard', 'context'))
- grad_b_qkv: float32 [2048], P(('shard', 'context'))
- grad_w_out: float32 [1536, 1536], P(('shard', 'context'))
- grad_ffn_gain: float32 [1536], P(('shard', 'context'))
- grad_w_gate_up: float32 [1536, 2, 8960], P('shard', None, 'context')
- grad_w_down: float32 [8960, 1536], P('context', 'shard')
Inputs may be any that keep to these rules, and one draw needn't show every extreme that they name: `segments`: segment numbers start at 0 in every sequence, never fall along it (a number may be skipped), and the last token of every sequence has 3. `positions`: a token's position is its index minus the index of the first token of its segment.
All inputs are finite; a program needn't handle non-finite values.
Results may differ from a plain program's by a relative error of at most 0.015.
Values may be sent and summed in bfloat16 or wider, within the bound.
No kernel may reach another device: no remote copies, remote signals or barrier semaphores. Data moves between devices by JAX's collectives and lax.ppermute only.
A program may use at most 192 MiB of HBM per device.

v0:
```python
import jax
import jax.numpy as jnp
from jax import lax
from jax.sharding import PartitionSpec as P

D = 1536
HEADS_Q = 12
HEADS_KV = 2
HEAD_DIM = 128
EPS = 1e-06
THETA = 1000000.0
NEG = -1e30


def shifted(block, axis, distance):
    devices = range(lax.axis_size(axis))
    route = [((i - distance) % len(devices), i) for i in devices]
    return lax.ppermute(block, axis, route)


def rope_tables(positions, head_size):
    half = head_size // 2
    frequency = THETA ** (-(jnp.arange(half, dtype=jnp.float32) * (2.0 / head_size)))
    angle = positions.astype(jnp.float32)[:, None] * frequency[None, :]
    cosine = jnp.cos(angle)
    sine_part = jnp.sin(angle)
    return (jnp.concatenate([cosine, cosine], 1), jnp.concatenate([sine_part, sine_part], 1))


def rotate(values, cosine, sine_part):
    half = values.shape[-1] // 2
    turned = jnp.concatenate([-values[..., half:], values[..., :half]], -1)
    return values * cosine[:, None, :] + turned * sine_part[:, None, :]


def unrotate(grads, cosine, sine_part):
    half = grads.shape[-1] // 2
    scaled = grads * sine_part[:, None, :]
    return grads * cosine[:, None, :] + jnp.concatenate(
        [scaled[..., half:], -scaled[..., :half]], -1
    )


def norm_back(values, inverse, weighted):
    return inverse * weighted - values * inverse**3 * jnp.mean(
        weighted * values, axis=-1, keepdims=True
    )


def block_scores(query, piece, start, query_index, query_seg, scale):
    keys, values, key_seg = piece
    key_index = start + jnp.arange(keys.shape[0], dtype=jnp.int32)
    scores = jnp.einsum("bhgd,jhd->hgbj", query, keys, preferred_element_type=jnp.float32) * scale
    allowed = (key_index[None, :] <= query_index[:, None]) & (
        key_seg[None, :] == query_seg[:, None]
    )
    return (jnp.where(allowed[None, None], scores, NEG), allowed)


def stats_update(carry, piece, start, query, query_index, query_seg, scale):
    best, total = carry
    scores, allowed = block_scores(query, piece, start, query_index, query_seg, scale)
    new_best = jnp.maximum(best, jnp.max(scores, axis=-1))
    factor = jnp.exp(best - new_best)
    weights = jnp.where(allowed[None, None], jnp.exp(scores - new_best[..., None]), 0.0)
    return (new_best, total * factor + jnp.sum(weights, axis=-1))


def attend_update(accum, piece, start, query, lse, query_index, query_seg, scale):
    scores, allowed = block_scores(query, piece, start, query_index, query_seg, scale)
    probs = jnp.where(allowed[None, None], jnp.exp(scores - lse[..., None]), 0.0).astype(
        jnp.bfloat16
    )
    return accum + jnp.einsum("hgbj,jhd->hgbd", probs, piece[1], preferred_element_type=jnp.float32)


def backward_update(piece, start, query, grad_grouped, lse, delta, query_index, query_seg, scale):
    keys, values, key_seg = piece
    scores, allowed = block_scores(query, piece, start, query_index, query_seg, scale)
    probs = jnp.where(allowed[None, None], jnp.exp(scores - lse[..., None]), 0.0)
    grad_values = jnp.einsum(
        "hgbj,bhgd->jhd",
        probs.astype(jnp.bfloat16),
        grad_grouped,
        preferred_element_type=jnp.float32,
    )
    grad_probs = jnp.einsum(
        "bhgd,jhd->hgbj", grad_grouped, values, preferred_element_type=jnp.float32
    )
    grad_scores = (probs * (grad_probs - delta[..., None])).astype(jnp.bfloat16)
    grad_query = (
        jnp.einsum("hgbj,jhd->bhgd", grad_scores, keys, preferred_element_type=jnp.float32) * scale
    )
    grad_keys = (
        jnp.einsum("hgbj,bhgd->jhd", grad_scores, query, preferred_element_type=jnp.float32) * scale
    )
    return (grad_query, grad_keys, grad_values)


def swiglu_forward(normed, gate_up_weight, down_weight):
    units = down_weight.shape[0]
    both = jnp.dot(
        normed,
        gate_up_weight.reshape(gate_up_weight.shape[0], 2 * units),
        preferred_element_type=jnp.float32,
    )
    gate = both[:, :units]
    upper = both[:, units:]
    sigma = jax.nn.sigmoid(gate)
    activated = gate * sigma
    hidden = (activated * upper).astype(jnp.bfloat16)
    return (gate, upper, sigma, activated, hidden)


def swiglu_grads(cot_rows, down_weight, gate, upper, sigma, activated):
    grad_hidden = jnp.dot(cot_rows, down_weight.T, preferred_element_type=jnp.float32)
    grad_gate = grad_hidden * upper * sigma * (1.0 + gate * (1.0 - sigma))
    grad_upper = grad_hidden * activated
    return jnp.concatenate([grad_gate, grad_upper], 1).astype(jnp.bfloat16)


def body(
    tokens,
    segments,
    positions,
    attn_gain,
    w_qkv,
    b_qkv,
    w_out,
    ffn_gain,
    w_gate_up,
    w_down,
    cotangent,
):
    rows = tokens.shape[0]
    group = HEADS_Q // HEADS_KV
    q_width = HEADS_Q * HEAD_DIM
    kv_width = HEADS_KV * HEAD_DIM
    scale = HEAD_DIM ** (-0.5)
    length = lax.axis_size("context")
    place = lax.axis_index("context")
    query_index = place * rows + jnp.arange(rows, dtype=jnp.int32)
    query_seg = segments.astype(jnp.bfloat16)
    qkv_full, out_full = (
        lax.all_gather(w_qkv, "shard", axis=0, tiled=True),
        lax.all_gather(w_out, "shard", axis=0, tiled=True),
    )
    tokens_wide = tokens.astype(jnp.float32)
    inverse_one = lax.rsqrt(jnp.mean(tokens_wide * tokens_wide, axis=-1, keepdims=True) + EPS)
    normed_one = (tokens_wide * inverse_one * attn_gain).astype(jnp.bfloat16)
    projected = jnp.dot(normed_one, qkv_full, preferred_element_type=jnp.float32) + b_qkv
    cosine, sine_part = rope_tables(positions, HEAD_DIM)
    query = rotate(
        projected[:, :q_width].reshape(rows, HEADS_Q, HEAD_DIM), cosine, sine_part
    ).astype(jnp.bfloat16)
    keys = rotate(
        projected[:, q_width : q_width + kv_width].reshape(rows, HEADS_KV, HEAD_DIM),
        cosine,
        sine_part,
    ).astype(jnp.bfloat16)
    values = (
        projected[:, q_width + kv_width :].reshape(rows, HEADS_KV, HEAD_DIM).astype(jnp.bfloat16)
    )
    grouped = query.reshape(rows, HEADS_KV, group, HEAD_DIM)
    own = (keys, values, query_seg)

    def cycle_pass(update, init):

        def pass_step(step, state):
            carry, held = state
            source = (place + step) % length
            carry = update(carry, held, source * rows)
            held = shifted((held[0], held[1], held[2]), "context", -1)
            return (carry, held)

        return lax.fori_loop(0, length, pass_step, (init, own))[0]

    stats_init = (
        jnp.full((HEADS_KV, group, rows), NEG, jnp.float32),
        jnp.zeros((HEADS_KV, group, rows), jnp.float32),
    )
    best, total = cycle_pass(
        lambda carry, piece, start: stats_update(
            carry, piece, start, grouped, query_index, query_seg, scale
        ),
        stats_init,
    )
    lse = best + jnp.log(total)
    accum = cycle_pass(
        lambda carry, piece, start: attend_update(
            carry, piece, start, grouped, lse, query_index, query_seg, scale
        ),
        jnp.zeros((HEADS_KV, group, rows, HEAD_DIM), jnp.float32),
    )
    attended = jnp.transpose(accum, (2, 0, 1, 3)).reshape(rows, q_width).astype(jnp.bfloat16)
    mixed = tokens_wide + jnp.dot(attended, out_full, preferred_element_type=jnp.float32)
    inverse_two = lax.rsqrt(jnp.mean(mixed * mixed, axis=-1, keepdims=True) + EPS)
    normed_two = (mixed * inverse_two * ffn_gain).astype(jnp.bfloat16)
    gate_up_part, down_part = (
        lax.all_gather(w_gate_up, "shard", axis=0, tiled=True),
        lax.all_gather(w_down, "shard", axis=1, tiled=True),
    )
    normed_all, cot_all = (
        lax.all_gather(normed_two, "context", axis=0, tiled=True),
        lax.all_gather(cotangent, "context", axis=0, tiled=True),
    )
    gate, upper, sigma, activated, hidden = swiglu_forward(normed_all, gate_up_part, down_part)
    down_rows = lax.psum_scatter(
        jnp.dot(hidden, down_part, preferred_element_type=jnp.float32).astype(jnp.bfloat16),
        "context",
        scatter_dimension=0,
        tiled=True,
    ).astype(jnp.float32)
    output = mixed + down_rows
    down_grad_part = jnp.dot(hidden.T, cot_all, preferred_element_type=jnp.float32)
    grad_both = swiglu_grads(cot_all, down_part, gate, upper, sigma, activated)
    units = down_part.shape[0]
    gate_up_grad_part = jnp.dot(
        normed_all.T, grad_both, preferred_element_type=jnp.float32
    ).reshape(D, 2, units)
    gate_up_flat = gate_up_part.reshape(D, 2 * units)
    grad_normed_two = lax.psum_scatter(
        jnp.dot(grad_both, gate_up_flat.T, preferred_element_type=jnp.float32),
        "context",
        scatter_dimension=0,
        tiled=True,
    )
    grad_gate_up, grad_down = (
        lax.psum_scatter(
            gate_up_grad_part.astype(jnp.bfloat16), "shard", scatter_dimension=0, tiled=True
        ).astype(jnp.float32),
        lax.psum_scatter(
            down_grad_part.astype(jnp.bfloat16), "shard", scatter_dimension=1, tiled=True
        ).astype(jnp.float32),
    )
    gain_two_term = jnp.sum(grad_normed_two * mixed * inverse_two, axis=0)
    grad_mixed = cotangent.astype(jnp.float32) + norm_back(
        mixed, inverse_two, grad_normed_two * ffn_gain
    )
    grad_mixed_low = grad_mixed.astype(jnp.bfloat16)
    out_term = jnp.dot(attended.T, grad_mixed_low, preferred_element_type=jnp.float32)
    grad_attended = jnp.dot(grad_mixed_low, out_full.T, preferred_element_type=jnp.float32).astype(
        jnp.bfloat16
    )
    grad_grouped = grad_attended.reshape(rows, HEADS_KV, group, HEAD_DIM)
    attended_grouped = attended.reshape(rows, HEADS_KV, group, HEAD_DIM)
    delta = jnp.transpose(
        jnp.sum(grad_grouped.astype(jnp.float32) * attended_grouped.astype(jnp.float32), axis=-1),
        (1, 2, 0),
    )
    zero_query = jnp.zeros((rows, HEADS_KV, group, HEAD_DIM), jnp.float32)
    zero_keys = jnp.zeros((rows, HEADS_KV, HEAD_DIM), jnp.float32)

    def back_step(step, state):
        grad_query, held, carried = state
        source = (place + step) % length
        part_query, part_keys, part_values = backward_update(
            held, source * rows, grouped, grad_grouped, lse, delta, query_index, query_seg, scale
        )
        carried = (carried[0] + part_keys, carried[1] + part_values)
        held = shifted((held[0], held[1], held[2]), "context", -1)
        carried = (
            shifted(carried[0].astype(jnp.bfloat16), "context", -1).astype(jnp.float32),
            shifted(carried[1].astype(jnp.bfloat16), "context", -1).astype(jnp.float32),
        )
        return (grad_query + part_query, held, carried)

    grad_query, _, (grad_keys, grad_values) = lax.fori_loop(
        0, length, back_step, (zero_query, own, (zero_keys, zero_keys))
    )
    grad_q = unrotate(grad_query.reshape(rows, HEADS_Q, HEAD_DIM), cosine, sine_part).reshape(
        rows, q_width
    )
    grad_k = unrotate(grad_keys, cosine, sine_part).reshape(rows, kv_width)
    grad_projected = jnp.concatenate([grad_q, grad_k, grad_values.reshape(rows, kv_width)], 1)
    bias_term = jnp.sum(grad_projected, axis=0)
    grad_projected_low = grad_projected.astype(jnp.bfloat16)
    qkv_term = jnp.dot(normed_one.T, grad_projected_low, preferred_element_type=jnp.float32)
    grad_normed_one = jnp.dot(grad_projected_low, qkv_full.T, preferred_element_type=jnp.float32)
    gain_one_term = jnp.sum(grad_normed_one * tokens_wide * inverse_one, axis=0)
    grad_tokens = grad_mixed + norm_back(tokens_wide, inverse_one, grad_normed_one * attn_gain)
    summed = (
        lax.psum_scatter(gain_one_term, ("shard", "context"), scatter_dimension=0, tiled=True),
        lax.psum_scatter(qkv_term, ("shard", "context"), scatter_dimension=0, tiled=True),
        lax.psum_scatter(bias_term, ("shard", "context"), scatter_dimension=0, tiled=True),
        lax.psum_scatter(out_term, ("shard", "context"), scatter_dimension=0, tiled=True),
        lax.psum_scatter(gain_two_term, ("shard", "context"), scatter_dimension=0, tiled=True),
    )
    return (
        output,
        grad_tokens,
        summed[0],
        summed[1],
        summed[2],
        summed[3],
        summed[4],
        grad_gate_up,
        grad_down,
    )


def solution(mesh):
    return jax.shard_map(
        body,
        mesh=mesh,
        in_specs=(
            P(("shard", "context"), None),
            P(("shard", "context")),
            P(("shard", "context")),
            P(),
            P("shard", None),
            P(),
            P("shard", None),
            P(),
            P("shard", None, "context"),
            P("context", "shard"),
            P(("shard", "context"), None),
        ),
        out_specs=(
            P(("shard", "context"), None),
            P(("shard", "context"), None),
            P(("shard", "context")),
            P(("shard", "context"), None),
            P(("shard", "context")),
            P(("shard", "context"), None),
            P(("shard", "context")),
            P("shard", None, "context"),
            P("context", "shard"),
        ),
        check_vma=False,
    )
```

profile of v0, /device:TPU:0, one launch (start us, length us, event | category | flops | bytes accessed | tf_op | source)
XLA Modules:
  0.0 918.2 jit_solution(16799553422252278018)
XLA Ops:
  13.0 69.7 %all-gather.7.cloned.1.call-done = bf16[1536,2048]{1,0:T(8,128)(2,1)} async-done(((bf16[384,2048]{1,0:T(8,128)(2,1)}), bf16[1536,2048]{1,0:T(8,128)(2,1)}) %all-gather.7.cloned.1.call-update) | async-done | bytes 6291472 | tf_op jit(solution)/shard_map/all_gather | solution.py:145
  82.7 3.8 convolution_add_fusion.2
  87.7 44.2 %while.70 = (s32[]{:T(128)}, f32[2,6,128]{2,1,0:T(8,128)S(1)}, f32[2,6,128]{2,1,0:T(8,128)S(1)}, bf16[128,2,128]{2,0,1:T(8,128)(2,1)S(1)}, bf16[128]{0:T(256)(12...) while((s32[]{:T(128)}, f32[2,6,128]{2,1,0:T(8,128)S(1)}, ...), condition=%wide.region_4.5_spmd.clone, body=%wide.region_1.4_spmd.clone.sunk | while | flops 51601168 | bytes 2558317 | solution.py:176
  87.7 2.6 collective-permute-start
  92.5 3.5 collective-permute-start
  98.0 3.7 collective-permute-start
  103.6 3.7 collective-permute-start
  109.3 3.7 collective-permute-start
  114.9 3.7 collective-permute-start
  120.6 3.7 collective-permute-start
  126.2 3.7 collective-permute-start
  132.4 50.7 %while.71 = (s32[]{:T(128)}, f32[2,6,128,128]{3,2,1,0:T(8,128)S(1)}, bf16[128,2,128]{2,0,1:T(8,128)(2,1)S(1)}, bf16[128,2,128]{2,0,1:T(8,128)(2,1)S(1)}, bf16[12...) while((s32[]{:T(128)}, ...), condition=%wide.region_6.7_spmd.clone, body=%wide.region_5.6_spmd.clone.sunk | while | flops 102121744 | bytes 2927004 | solution.py:176
  132.5 3.7 collective-permute-start.2
  138.7 3.8 collective-permute-start.2
  145.1 3.8 collective-permute-start.2
  151.4 3.8 collective-permute-start.2
  157.8 3.8 collective-permute-start.2
  164.1 3.8 collective-permute-start.2
  170.5 3.8 collective-permute-start.2
  176.8 3.8 collective-permute-start.2
  183.4 3.6 multiply_reduce_fusion.3
  190.1 28.0 %all-gather.13.cloned.1.call-done = bf16[1536,2,1120]{0,2,1:T(8,128)(2,1)} async-done(((bf16[384,2,1120]{0,2,1:T(8,128)(2,1)}), bf16[1536,2,1120]{0,2,1:T(8,128)(2,1)}) %all-gather.13.cloned.1.call-update) | async-done | bytes 6881296 | tf_op jit(solution)/shard_map/all_gather | solution.py:200
  218.1 40.3 %all-gather.11.cloned.1.call-done = bf16[1024,1536]{1,0:T(8,128)(2,1)} async-done(((bf16[128,1536]{1,0:T(8,128)(2,1)}), bf16[1024,1536]{1,0:T(8,128)(2,1)}) %all-gather.11.cloned.1.call-update) | async-done | bytes 3145744 | tf_op jit(solution)/shard_map/all_gather | solution.py:204
  258.4 12.6 %fusion.79 = f32[1024,2240]{0,1:T(8,128)} fusion(bf16[1024,1536]{1,0:T(8,128)(2,1)} %all-gather.11.cloned.1.call-done, bf16[1536,2240]{0,1:T(8,128)(2,1)} %bitcast.218), kind=kOutput, calls=%fused_computation.141 | convolution fusion | flops 7046430720 | bytes 19202048 | tf_op jit(solution)/shard_map/dot_general | solution.py:102
  271.1 34.1 %all-gather.15.cloned.1.call-done = bf16[1120,1536]{1,0:T(8,128)(2,1)} async-done(((bf16[1120,384]{1,0:T(8,128)(2,1)}), bf16[1120,1536]{1,0:T(8,128)(2,1)}) %all-gather.15.cloned.1.call-update) | async-done | bytes 3440656 | tf_op jit(solution)/shard_map/all_gather | solution.py:201
  305.2 39.7 %all-gather.17.cloned.1.call-done = bf16[1024,1536]{1,0:T(8,128)(2,1)} async-done(((bf16[128,1536]{1,0:T(8,128)(2,1)}), bf16[1024,1536]{1,0:T(8,128)(2,1)}) %all-gather.17.cloned.1.call-update) | async-done | bytes 3145744 | tf_op jit(solution)/shard_map/all_gather | solution.py:205
  345.0 12.4 %multiply_convert_fusion.1 = (bf16[1024,1120]{0,1:T(8,128)(2,1)S(1)}, bf16[1024,1120]{0,1:T(8,128)(2,1)S(1)}, bf16[1024,1120]{0,1:T(8,128)(2,1)}) fusion(f32[1024,2240]{0,1:T(8,128)} %fusion.79, bf16[1024,1536]{1,0:T(8,128)(2,1)} %all-gather.17.cloned.1.call-done, bf16[1120,1536]{1,0:T(8,128)(2,1)} %all-gather.15.cloned.1.call-done), kind=kOutput, calls=%fused_computation.67 | convolution fusion | flops 3540418560 | bytes 22642688 | tf_op jit(solution)/shard_map/dot_general | solution.py:116
  359.5 9.6 %fusion.48 = f32[1024,1536]{1,0:T(8,128)} fusion(bf16[1536,2240]{0,1:T(8,128)(2,1)S(1)} %bitcast.219, bf16[1024,1120]{0,1:T(8,128)(2,1)S(1)} %get-tuple-element.1096, bf16[1024,1120]{0,1:T(8,128)(2,1)S(1)} %get-tuple-element.1095), kind=kOutput, calls=%fused_computation.72 | convolution fusion | flops 7055605760 | bytes 17760256 | tf_op jit(solution)/shard_map/dot_general | solution.py:223
  369.3 8.7 convolution_convert_fusion.2
  378.0 8.1 convolution_convert_fusion.1
  386.1 5.7 copy.89
  391.8 12.2 %convolution_convert_fusion = bf16[1536,2240]{0,1:T(8,128)(2,1)} fusion(bf16[1024,1536]{1,0:T(8,128)(2,1)} %all-gather.11.cloned.1.call-done, bf16[1024,1120]{0,1:T(8,128)(2,1)} %copy-done.19, bf16[1024,1120]{0,1:T(8,128)(2,1)} %copy-done.18), kind=kOutput, calls=%fused_computation.63 | convolution fusion | flops 7059046400 | bytes 14614528 | tf_op jit(solution)/shard_map/dot_general | solution.py:218
  404.0 9.9 %copy.92 = bf16[1536,2240]{1,0:T(8,128)(2,1)} copy(bf16[1536,2240]{0,1:T(8,128)(2,1)} %convolution_convert_fusion) | data formatting | bytes 13762560
  415.4 22.4 %reduce-scatter.13.cloned.1.call-done = f32[128,1536]{1,0:T(8,128)} async-done(((f32[1024,1536]{1,0:T(8,128)}), f32[128,1536]{1,0:T(8,128)}) %reduce-scatter.13.cloned.1.call-update) | async-done | bytes 786448 | tf_op jit(solution)/shard_map/reduce_scatter | solution.py:222
  437.8 2.0 multiply_reduce_fusion
  440.3 38.7 %reduce-scatter.11.cloned.1.call-done = bf16[128,1536]{1,0:T(8,128)(2,1)} async-done(((bf16[1024,1536]{1,0:T(8,128)(2,1)}), bf16[128,1536]{1,0:T(8,128)(2,1)}) %reduce-scatter.11.cloned.1.call-update) | async-done | bytes 393232 | tf_op jit(solution)/shard_map/reduce_scatter | solution.py:208
  479.0 2.6 subtract_add_fusion
  481.6 4.0 convolution_convert_fusion.3
  489.0 5.0 fusion.62
  494.0 90.0 %while.72 = (s32[]{:T(128)}, f32[128,2,6,128]{3,0,2,1:T(8,128)S(1)}, bf16[128,2,128]{2,0,1:T(8,128)(2,1)S(1)}, bf16[128,2,128]{2,0,1:T(8,128)(2,1)S(1)}, bf16[12...) while((s32[]{:T(128)}, ...), condition=%wide.region_13.14_spmd.clone, body=%wide.region_12.13_spmd.clone.sunk | while | flops 254198032 | bytes 9028110 | solution.py:268
  494.0 1.6 collective-permute-start.5
  502.0 3.7 collective-permute-start.5
  510.9 2.3 collective-permute-start.9
  513.6 1.5 collective-permute-done.9
  515.1 3.6 collective-permute-start.5
  525.1 3.7 collective-permute-start.5
  534.0 1.9 collective-permute-start.9
  536.3 1.5 collective-permute-done.9
  537.8 3.6 collective-permute-start.5
  547.9 3.6 collective-permute-start.5
  556.7 2.2 collective-permute-start.9
  559.4 1.5 collective-permute-done.9
  560.9 3.6 collective-permute-start.5
  571.0 3.6 collective-permute-start.5
  579.8 2.2 collective-permute-start.9
  582.5 1.5 collective-permute-done.9
  585.8 6.4 fusion.67
  592.3 2.3 copy.90
  596.3 5.2 fusion.57
  601.5 39.4 %all-reduce.3 = (f32[1536]{0:T(1024)S(1)}, f32[2048]{0:T(1024)S(1)}, f32[1536]{0:T(1024)S(1)}) all-reduce(f32[1536]{0:T(1024)S(1)} %get-tuple-element.1022, f32[2048]{0:T(1024)S(1)} %fusion.60, f32[1536]{0:T(1024)S(1)} %copy-done.10), channel_id=4, replica_groups=mesh['shard'=4,'context'=8] {'shard','context'}, use_global_device_ids=true, to_apply=%region_16.17.clone | all-reduce | flops 5120 | bytes 40960
  643.9 2.8 copy.93
  646.7 2.0 convert_element_type.173
  648.7 102.1 %reduce-scatter.17.cloned.1.call-done = f32[48,1536]{1,0:T(8,128)} async-done(((f32[1536,1536]{1,0:T(8,128)}), f32[48,1536]{1,0:T(8,128)}) %reduce-scatter.17.cloned.1.call-update) | async-done | bytes 294928 | tf_op jit(solution)/shard_map/reduce_scatter | solution.py:286
  750.8 160.3 %reduce-scatter.15.cloned.1.call-done = f32[48,2048]{1,0:T(8,128)} async-done(((f32[1536,2048]{1,0:T(8,128)}), f32[48,2048]{1,0:T(8,128)}) %reduce-scatter.15.cloned.1.call-update) | async-done | bytes 393232 | tf_op jit(solution)/shard_map/reduce_scatter | solution.py:284
  (491 shorter events, 108.1 us)
Async XLA Ops:
  7.2 75.4 %all-gather.7.cloned.1.call-start = ((), (), s32[]{:S(2)}) async-start(), calls=%async_computation.6 | async-start | bytes 7864320 | tf_op jit(solution)/shard_map/all_gather | solution.py:145
  8.0 175.5 %all-gather.9.cloned.1.call-start = ((), (), s32[]{:S(2)}) async-start(), calls=%async_computation.7 | async-start | bytes 5898240 | tf_op jit(solution)/shard_map/all_gather | solution.py:146
  8.7 209.4 %all-gather.13.cloned.1.call-start = ((), (), s32[]{:S(2)}) async-start(), calls=%async_computation.9 | async-start | bytes 8601600 | tf_op jit(solution)/shard_map/all_gather | solution.py:200
  9.4 249.0 %all-gather.11.cloned.1.call-start = ((), (), s32[]{:S(2)}) async-start(), calls=%async_computation.8 | async-start | bytes 3538944 | tf_op jit(solution)/shard_map/all_gather | solution.py:204
  87.7 4.8 collective-permute-start
  92.5 5.5 collective-permute-start
  98.0 5.6 collective-permute-start
  103.6 5.6 collective-permute-start
  109.3 5.6 collective-permute-start
  114.9 5.6 collective-permute-start
  120.6 5.6 collective-permute-start
  126.2 5.6 collective-permute-start
  132.5 6.3 collective-permute-start.2
  136.1 2.6 collective-permute-start.3
  138.7 6.3 collective-permute-start.2
  142.5 2.6 collective-permute-start.3
  145.1 6.3 collective-permute-start.2
  148.8 2.6 collective-permute-start.3
  151.4 6.3 collective-permute-start.2
  155.2 2.6 collective-permute-start.3
  157.8 6.3 collective-permute-start.2
  164.1 6.3 collective-permute-start.2
  170.5 6.3 collective-permute-start.2
  176.8 6.3 collective-permute-start.2
  188.4 116.8 %all-gather.15.cloned.1.call-start = ((), (), s32[]{:S(2)}) async-start(), calls=%async_computation.10 | async-start | bytes 4300800 | tf_op jit(solution)/shard_map/all_gather | solution.py:201
  189.0 155.9 %all-gather.17.cloned.1.call-start = ((), (), s32[]{:S(2)}) async-start(), calls=%async_computation.12 | async-start | bytes 3538944 | tf_op jit(solution)/shard_map/all_gather | solution.py:205
  189.6 248.2 %reduce-scatter.13.cloned.1.call-start = ((), (), s32[]{:S(2)}) async-start(), calls=%async_computation.13 | async-start | bytes 7077888 | tf_op jit(solution)/shard_map/reduce_scatter | solution.py:222
  369.0 109.9 %reduce-scatter.11.cloned.1.call-start = ((), (), s32[]{:S(2)}) async-start(), calls=%async_computation.11 | async-start | bytes 3538944 | tf_op jit(solution)/shard_map/reduce_scatter | solution.py:208
  377.9 214.4 %reduce-scatter.21.cloned.1.call-start = ((), (), s32[]{:S(2)}) async-start(), calls=%async_computation.17 | async-start | bytes 4423680
  391.7 252.1 %reduce-scatter.19.cloned.1.call-start = ((), (), s32[]{:S(2)}) async-start(), calls=%async_computation.16 | async-start | bytes 8847360
  413.9 336.9 %reduce-scatter.17.cloned.1.call-start = ((), (), s32[]{:S(2)}) async-start(), calls=%async_computation.15 | async-start | bytes 9732096 | tf_op jit(solution)/shard_map/reduce_scatter | solution.py:286
  493.9 417.2 %reduce-scatter.15.cloned.1.call-start = ((), (), s32[]{:S(2)}) async-start(), calls=%async_computation.14 | async-start | bytes 12976128 | tf_op jit(solution)/shard_map/reduce_scatter | solution.py:284
  494.0 7.9 collective-permute-start.5
  495.7 6.3 collective-permute-start.6
  496.9 5.0 collective-permute-start.7
  502.0 13.1 %collective-permute-start.5 = (bf16[128,2,128]{2,0,1:T(8,128)(2,1)S(1)}, bf16[128,2,128]{2,0,1:T(8,128)(2,1)S(1)}, u32[]{:S(2)}, u32[]{:S(2)}) collective-permute-start(bf16[128,2,128]{2,0,1:T(8,128)(2,1)S(1)} %copy.135), channel_id=1, source_target_pairs={{1,0},{2,1},{3,2},{4,3},{5,4},{6,5},{7,6},{0,7},{9,8},{10,9},{11,1... | collective-permute-start | bytes 196616 | tf_op jit(solution)/shard_map/while/body/eval_jaxpr/ppermute | solution.py:18
  505.7 9.4 %collective-permute-start.6 = (bf16[128,2,128]{2,0,1:T(8,128)(2,1)S(1)}, bf16[128,2,128]{2,0,1:T(8,128)(2,1)S(1)}, u32[]{:S(2)}, u32[]{:S(2)}) collective-permute-start(bf16[128,2,128]{2,0,1:T(8,128)(2,1)S(1)} %copy.136), channel_id=1, source_target_pairs={{1,0},{2,1},{3,2},{4,3},{5,4},{6,5},{7,6},{0,7},{9,8},{10,9},{11,1... | collective-permute-start | bytes 196616 | tf_op jit(solution)/shard_map/while/body/eval_jaxpr/ppermute | solution.py:18
  507.0 8.1 collective-permute-start.7
  509.3 4.2 collective-permute-start.8
  510.9 4.2 collective-permute-start.9
  515.1 9.9 %collective-permute-start.5 = (bf16[128,2,128]{2,0,1:T(8,128)(2,1)S(1)}, bf16[128,2,128]{2,0,1:T(8,128)(2,1)S(1)}, u32[]{:S(2)}, u32[]{:S(2)}) collective-permute-start(bf16[128,2,128]{2,0,1:T(8,128)(2,1)S(1)} %copy.135), channel_id=1, source_target_pairs={{1,0},{2,1},{3,2},{4,3},{5,4},{6,5},{7,6},{0,7},{9,8},{10,9},{11,1... | collective-permute-start | bytes 196616 | tf_op jit(solution)/shard_map/while/body/eval_jaxpr/ppermute | solution.py:18
  518.8 6.3 collective-permute-start.6
  520.0 5.0 collective-permute-start.7
  525.1 12.7 %collective-permute-start.5 = (bf16[128,2,128]{2,0,1:T(8,128)(2,1)S(1)}, bf16[128,2,128]{2,0,1:T(8,128)(2,1)S(1)}, u32[]{:S(2)}, u32[]{:S(2)}) collective-permute-start(bf16[128,2,128]{2,0,1:T(8,128)(2,1)S(1)} %copy.135), channel_id=1, source_target_pairs={{1,0},{2,1},{3,2},{4,3},{5,4},{6,5},{7,6},{0,7},{9,8},{10,9},{11,1... | collective-permute-start | bytes 196616 | tf_op jit(solution)/shard_map/while/body/eval_jaxpr/ppermute | solution.py:18
  528.8 9.0 collective-permute-start.6
  530.1 7.7 collective-permute-start.7
  532.5 3.8 collective-permute-start.8
  534.0 3.8 collective-permute-start.9
  537.8 10.0 %collective-permute-start.5 = (bf16[128,2,128]{2,0,1:T(8,128)(2,1)S(1)}, bf16[128,2,128]{2,0,1:T(8,128)(2,1)S(1)}, u32[]{:S(2)}, u32[]{:S(2)}) collective-permute-start(bf16[128,2,128]{2,0,1:T(8,128)(2,1)S(1)} %copy.135), channel_id=1, source_target_pairs={{1,0},{2,1},{3,2},{4,3},{5,4},{6,5},{7,6},{0,7},{9,8},{10,9},{11,1... | collective-permute-start | bytes 196616 | tf_op jit(solution)/shard_map/while/body/eval_jaxpr/ppermute | solution.py:18
  541.5 6.4 collective-permute-start.6
  542.7 5.1 collective-permute-start.7
  547.9 13.0 %collective-permute-start.5 = (bf16[128,2,128]{2,0,1:T(8,128)(2,1)S(1)}, bf16[128,2,128]{2,0,1:T(8,128)(2,1)S(1)}, u32[]{:S(2)}, u32[]{:S(2)}) collective-permute-start(bf16[128,2,128]{2,0,1:T(8,128)(2,1)S(1)} %copy.135), channel_id=1, source_target_pairs={{1,0},{2,1},{3,2},{4,3},{5,4},{6,5},{7,6},{0,7},{9,8},{10,9},{11,1... | collective-permute-start | bytes 196616 | tf_op jit(solution)/shard_map/while/body/eval_jaxpr/ppermute | solution.py:18
  551.5 9.4 %collective-permute-start.6 = (bf16[128,2,128]{2,0,1:T(8,128)(2,1)S(1)}, bf16[128,2,128]{2,0,1:T(8,128)(2,1)S(1)}, u32[]{:S(2)}, u32[]{:S(2)}) collective-permute-start(bf16[128,2,128]{2,0,1:T(8,128)(2,1)S(1)} %copy.136), channel_id=1, source_target_pairs={{1,0},{2,1},{3,2},{4,3},{5,4},{6,5},{7,6},{0,7},{9,8},{10,9},{11,1... | collective-permute-start | bytes 196616 | tf_op jit(solution)/shard_map/while/body/eval_jaxpr/ppermute | solution.py:18
  552.8 8.1 collective-permute-start.7
  555.2 4.2 collective-permute-start.8
  556.7 4.1 collective-permute-start.9
  560.9 10.0 %collective-permute-start.5 = (bf16[128,2,128]{2,0,1:T(8,128)(2,1)S(1)}, bf16[128,2,128]{2,0,1:T(8,128)(2,1)S(1)}, u32[]{:S(2)}, u32[]{:S(2)}) collective-permute-start(bf16[128,2,128]{2,0,1:T(8,128)(2,1)S(1)} %copy.135), channel_id=1, source_target_pairs={{1,0},{2,1},{3,2},{4,3},{5,4},{6,5},{7,6},{0,7},{9,8},{10,9},{11,1... | collective-permute-start | bytes 196616 | tf_op jit(solution)/shard_map/while/body/eval_jaxpr/ppermute | solution.py:18
  564.6 6.4 collective-permute-start.6
  565.8 5.1 collective-permute-start.7
  571.0 13.0 %collective-permute-start.5 = (bf16[128,2,128]{2,0,1:T(8,128)(2,1)S(1)}, bf16[128,2,128]{2,0,1:T(8,128)(2,1)S(1)}, u32[]{:S(2)}, u32[]{:S(2)}) collective-permute-start(bf16[128,2,128]{2,0,1:T(8,128)(2,1)S(1)} %copy.135), channel_id=1, source_target_pairs={{1,0},{2,1},{3,2},{4,3},{5,4},{6,5},{7,6},{0,7},{9,8},{10,9},{11,1... | collective-permute-start | bytes 196616 | tf_op jit(solution)/shard_map/while/body/eval_jaxpr/ppermute | solution.py:18
  574.6 9.4 %collective-permute-start.6 = (bf16[128,2,128]{2,0,1:T(8,128)(2,1)S(1)}, bf16[128,2,128]{2,0,1:T(8,128)(2,1)S(1)}, u32[]{:S(2)}, u32[]{:S(2)}) collective-permute-start(bf16[128,2,128]{2,0,1:T(8,128)(2,1)S(1)} %copy.136), channel_id=1, source_target_pairs={{1,0},{2,1},{3,2},{4,3},{5,4},{6,5},{7,6},{0,7},{9,8},{10,9},{11,1... | collective-permute-start | bytes 196616 | tf_op jit(solution)/shard_map/while/body/eval_jaxpr/ppermute | solution.py:18
  575.9 8.1 collective-permute-start.7
  578.3 4.2 collective-permute-start.8
  579.8 4.1 collective-permute-start.9
  (48 other events, 915.1 us)
Sparse Core Ops, SparseCore 0:
  9.9 72.7 all-gather.6
  84.5 56.9 all-gather.8
  143.3 74.7 all-gather.12
  220.2 38.2 all-gather.10
  260.1 45.0 all-gather.14
  306.7 38.2 all-gather.16
  369.2 68.6 reduce-scatter.12
  440.1 38.8 reduce-scatter.10
  482.1 46.4 reduce-scatter.20
  531.5 76.5 reduce-scatter.18
  614.5 136.2 reduce-scatter.16
  757.3 153.7 reduce-scatter.14
where the time goes:
time: 924 us; the launch traced here: 918 us
  waiting for transfers between devices  557 us (60%)
  matrix products  122 us (13%)
  starting transfers between devices  105 us (11%)
  local copies, waits for them, and re-layouts  40.6 us (4%)
  blocking collectives  39.4 us (4%)
  other arithmetic  36.7 us (4%)
  between operations  14.9 us (2%)
    reduce_scatter x1, waiting for transfers between devices, body(): lax.psum_scatter(qkv_term, ('shard', 'context'), scatter_dimension=0, til...  160 us
    ppermute x80, starting transfers between devices, shifted(): return lax.ppermute(block, axis, route)  104 us
    reduce_scatter x1, waiting for transfers between devices, body(): lax.psum_scatter(out_term, ('shard', 'context'), scatter_dimension=0, til...  102 us
    all_gather x1, waiting for transfers between devices, body(): lax.all_gather(w_qkv, 'shard', axis=0, tiled=True)  69.7 us
    all_gather x1, waiting for transfers between devices, body(): lax.all_gather(normed_two, 'context', axis=0, tiled=True)  40.3 us
    all_gather x1, waiting for transfers between devices, body(): lax.all_gather(cotangent, 'context', axis=0, tiled=True)  39.7 us
    unnamed x1, blocking collectives  39.4 us
    reduce_scatter x1, waiting for transfers between devices, body(): lax.psum_scatter(jnp.dot(hidden, down_part, preferred_element_type=jnp.fl...  38.7 us
  transfers between devices with their start and end apart: 92, of which 36 were waited for; matrix products, arithmetic and copies ran while one was open for 19% of the time, Pallas kernels for 0%

commit v1 on v0

--- a/solution.py
+++ b/solution.py
@@ -10,6 +10,24 @@
 EPS = 1e-06
 THETA = 1000000.0
 NEG = -1e30
+
+
+def ring_gather(array, axis, dim):
+    ways, here, lap = (lax.axis_size(axis), lax.axis_index(axis), array.shape[dim])
+    shape = [n * ways if d == dim else n for d, n in enumerate(array.shape)]
+    full = lax.dynamic_update_slice_in_dim(
+        jnp.zeros(shape, array.dtype), array, here * lap, axis=dim
+    )
+    going_up = going_down = array
+    for far in range(1, ways // 2 + 1):
+        going_up = lax.ppermute(going_up, axis, [(d, (d + 1) % ways) for d in range(ways)])
+        full = lax.dynamic_update_slice_in_dim(full, going_up, (here - far) % ways * lap, axis=dim)
+        if 2 * far < ways:
+            going_down = lax.ppermute(going_down, axis, [(d, (d - 1) % ways) for d in range(ways)])
+            full = lax.dynamic_update_slice_in_dim(
+                full, going_down, (here + far) % ways * lap, axis=dim
+            )
+    return full
 
 
 def shifted(block, axis, distance):
@@ -201,7 +219,7 @@
         lax.all_gather(w_down, "shard", axis=1, tiled=True),
     )
     normed_all, cot_all = (
-        lax.all_gather(normed_two, "context", axis=0, tiled=True),
+        ring_gather(normed_two, "context", 0),
         lax.all_gather(cotangent, "context", axis=0, tiled=True),
     )
     gate, upper, sigma, activated, hidden = swiglu_forward(normed_all, gate_up_part, down_part)

time: 924 us -> 886 us (0.959)
  waiting for transfers between devices: 557 us -> 500 us
  starting transfers between devices: 105 us -> 116 us
    all_gather x1 -> x0, waiting for transfers between devices: 40.3 us -> none  [body(): lax.all_gather(normed_two, 'context', axis=0, tiled=True)]
    ppermute x0 -> x7, waiting for transfers between devices: none -> 29.8 us  [the longest x4 29.8 us: ring_gather(): lax.ppermute(going_up, axis, [(d, (d + 1) % ways) for d in range(ways)])]
    all_gather x1, waiting for transfers between devices: 28 us -> 0.01 us  [body(): lax.all_gather(w_gate_up, 'shard', axis=0, tiled=True)]
    all_gather x1, waiting for transfers between devices: 34.1 us -> 16.9 us  [body(): lax.all_gather(w_down, 'shard', axis=1, tiled=True)]
    ppermute x0 -> x7, starting transfers between devices: none -> 11.3 us  [the longest x3 9.45 us: ring_gather(): lax.ppermute(going_down, axis, [(d, (d - 1) % ways) for d in range(ways)])]
    unnamed x57 -> x78, local copies, waits for them, and re-layouts: 28.8 us -> 32.2 us
  transfers between devices with their start and end apart: 92 -> 98, of which waited for: 36 -> 38; matrix products, arithmetic and copies ran while one was open for 19% -> 20% of each run, Pallas kernels for 0% -> 0%
where the time goes in v1:
time: 886 us; the launch traced here: 879 us
  waiting for transfers between devices  500 us (56%)
  matrix products  123 us (14%)
  starting transfers between devices  116 us (13%)
  local copies, waits for them, and re-layouts  49 us (6%)
  blocking collectives  39.2 us (4%)
  other arithmetic  35.5 us (4%)
  between operations  14.7 us (2%)
    reduce_scatter x1, waiting for transfers between devices, body(): lax.psum_scatter(qkv_term, ('shard', 'context'), scatter_dimension=0, til...  160 us
    ppermute x80, starting transfers between devices, shifted(): return lax.ppermute(block, axis, route)  104 us
    reduce_scatter x1, waiting for transfers between devices, body(): lax.psum_scatter(out_term, ('shard', 'context'), scatter_dimension=0, til...  102 us
    all_gather x1, waiting for transfers between devices, body(): lax.all_gather(w_qkv, 'shard', axis=0, tiled=True)  68.1 us
    all_gather x1, waiting for transfers between devices, body(): lax.all_gather(cotangent, 'context', axis=0, tiled=True)  39.7 us
    unnamed x1, blocking collectives  39.2 us
    reduce_scatter x1, waiting for transfers between devices, body(): lax.psum_scatter(jnp.dot(hidden, down_part, preferred_element_type=jnp.fl...  38.7 us
    unnamed x78, local copies, waits for them, and re-layouts  32.2 us
  transfers between devices with their start and end apart: 98, of which 38 were waited for; matrix products, arithmetic and copies ran while one was open for 20% of the time, Pallas kernels for 0%

profile of v1, /device:TPU:0, one launch (start us, length us, event | category | flops | bytes accessed | tf_op | source)
XLA Modules:
  0.0 878.8 jit_solution(9172420742360692012)
XLA Ops:
  14.6 68.1 %all-gather.6.cloned.1.call-done = bf16[1536,2048]{1,0:T(8,128)(2,1)} async-done(((bf16[384,2048]{1,0:T(8,128)(2,1)}), bf16[1536,2048]{1,0:T(8,128)(2,1)}) %all-gather.6.cloned.1.call-update) | async-done | bytes 6291472 | tf_op jit(solution)/shard_map/all_gather | solution.py:163
  82.7 3.8 convolution_add_fusion.2
  87.9 44.2 %while.70 = (s32[]{:T(128)}, f32[2,6,128]{2,1,0:T(8,128)S(1)}, f32[2,6,128]{2,1,0:T(8,128)S(1)}, bf16[128,2,128]{2,0,1:T(8,128)(2,1)S(1)}, bf16[128]{0:T(256)(12...) while((s32[]{:T(128)}, f32[2,6,128]{2,1,0:T(8,128)S(1)}, ...), condition=%wide.region_4.5_spmd.clone, body=%wide.region_1.4_spmd.clone.sunk | while | flops 51601168 | bytes 2558317 | solution.py:194
  88.0 2.7 collective-permute-start
  92.8 3.5 collective-permute-start
  98.3 3.7 collective-permute-start
  103.9 3.7 collective-permute-start
  109.6 3.7 collective-permute-start
  115.2 3.7 collective-permute-start
  120.9 3.7 collective-permute-start
  126.5 3.7 collective-permute-start
  132.7 50.7 %while.71 = (s32[]{:T(128)}, f32[2,6,128,128]{3,2,1,0:T(8,128)S(1)}, bf16[128,2,128]{2,0,1:T(8,128)(2,1)S(1)}, bf16[128,2,128]{2,0,1:T(8,128)(2,1)S(1)}, bf16[12...) while((s32[]{:T(128)}, ...), condition=%wide.region_6.7_spmd.clone, body=%wide.region_5.6_spmd.clone.sunk | while | flops 102121744 | bytes 2927004 | solution.py:194
  132.8 3.7 collective-permute-start.2
  139.0 3.8 collective-permute-start.2
  145.4 3.8 collective-permute-start.2
  151.7 3.8 collective-permute-start.2
  158.1 3.8 collective-permute-start.2
  164.4 3.8 collective-permute-start.2
  170.8 3.8 collective-permute-start.2
  177.1 3.8 collective-permute-start.2
  183.7 3.6 multiply_reduce_fusion.3
  191.2 2.4 collective-permute-start.11
  193.6 9.0 %collective-permute-done.10 = bf16[128,1536]{1,0:T(8,128)(2,1)S(1)} collective-permute-done((bf16[128,1536]{1,0:T(8,128)(2,1)S(1)}, bf16[128,1536]{1,0:T(8,128)(2,1)S(1)}, u32[]{:S(2)}, u32[]{:S(2)}) %collective-permute-start.10) | collective-permute-done | bytes 393248 | tf_op jit(solution)/shard_map/ppermute | solution.py:23
  202.5 3.5 collective-permute-start.13
  207.7 7.5 collective-permute-done.12
  215.1 3.5 collective-permute-start.15
  220.3 6.0 collective-permute-done.14
  228.3 7.4 collective-permute-done.16
  236.5 12.6 %fusion.79 = f32[1024,2240]{0,1:T(8,128)} fusion(bf16[1024,1536]{1,0:T(8,128)(2,1)} %constant_dynamic-update-slice_fusion, bf16[1536,2240]{0,1:T(8,128)(2,1)} %bitcast.218), kind=kOutput, calls=%fused_computation.149 | convolution fusion | flops 7046430720 | bytes 19202048 | tf_op jit(solution)/shard_map/dot_general | solution.py:120
  249.1 16.9 %all-gather.12.cloned.1.call-done = bf16[1120,1536]{1,0:T(8,128)(2,1)} async-done(((bf16[1120,384]{1,0:T(8,128)(2,1)}), bf16[1120,1536]{1,0:T(8,128)(2,1)}) %all-gather.12.cloned.1.call-update) | async-done | bytes 3440656 | tf_op jit(solution)/shard_map/all_gather | solution.py:219
  266.0 39.7 %all-gather.14.cloned.1.call-done = bf16[1024,1536]{1,0:T(8,128)(2,1)} async-done(((bf16[128,1536]{1,0:T(8,128)(2,1)}), bf16[1024,1536]{1,0:T(8,128)(2,1)}) %all-gather.14.cloned.1.call-update) | async-done | bytes 3145744 | tf_op jit(solution)/shard_map/all_gather | solution.py:223
  305.7 12.5 %multiply_convert_fusion.1 = (bf16[1024,1120]{0,1:T(8,128)(2,1)S(1)}, bf16[1024,1120]{0,1:T(8,128)(2,1)S(1)}, bf16[1024,1120]{0,1:T(8,128)(2,1)}) fusion(f32[1024,2240]{0,1:T(8,128)} %fusion.79, bf16[1024,1536]{1,0:T(8,128)(2,1)} %all-gather.14.cloned.1.call-done, bf16[1120,1536]{1,0:T(8,128)(2,1)} %all-gather.12.cloned.1.call-done), kind=kOutput, calls=%fused_computation.67 | convolution fusion | flops 3540418560 | bytes 22642688 | tf_op jit(solution)/shard_map/dot_general | solution.py:134
  320.3 9.6 %fusion.48 = f32[1024,1536]{1,0:T(8,128)} fusion(bf16[1536,2240]{0,1:T(8,128)(2,1)S(1)} %bitcast.219, bf16[1024,1120]{0,1:T(8,128)(2,1)S(1)} %get-tuple-element.1098, bf16[1024,1120]{0,1:T(8,128)(2,1)S(1)} %get-tuple-element.1097), kind=kOutput, calls=%fused_computation.72 | convolution fusion | flops 7055605760 | bytes 17760256 | tf_op jit(solution)/shard_map/dot_general | solution.py:241
  330.1 8.6 convolution_convert_fusion.2
  338.8 8.1 convolution_convert_fusion.1
  346.9 5.7 copy.89
  352.7 12.2 %convolution_convert_fusion = bf16[1536,2240]{0,1:T(8,128)(2,1)} fusion(bf16[1024,1536]{1,0:T(8,128)(2,1)} %constant_dynamic-update-slice_fusion, bf16[1024,1120]{0,1:T(8,128)(2,1)} %copy-done.30, bf16[1024,1120]{0,1:T(8,128)(2,1)} %copy-done.29), kind=kOutput, calls=%fused_computation.63 | convolution fusion | flops 7059046400 | bytes 14614528 | tf_op jit(solution)/shard_map/dot_general | solution.py:236
  364.9 10.3 %copy.92 = bf16[1536,2240]{1,0:T(8,128)(2,1)} copy(bf16[1536,2240]{0,1:T(8,128)(2,1)} %convolution_convert_fusion) | data formatting | bytes 13762560
  376.7 22.0 %reduce-scatter.13.cloned.1.call-done = f32[128,1536]{1,0:T(8,128)} async-done(((f32[1024,1536]{1,0:T(8,128)}), f32[128,1536]{1,0:T(8,128)}) %reduce-scatter.13.cloned.1.call-update) | async-done | bytes 786448 | tf_op jit(solution)/shard_map/reduce_scatter | solution.py:240
  401.2 38.7 %reduce-scatter.11.cloned.1.call-done = bf16[128,1536]{1,0:T(8,128)(2,1)} async-done(((bf16[1024,1536]{1,0:T(8,128)(2,1)}), bf16[128,1536]{1,0:T(8,128)(2,1)}) %reduce-scatter.11.cloned.1.call-update) | async-done | bytes 393232 | tf_op jit(solution)/shard_map/reduce_scatter | solution.py:226
  439.9 2.5 subtract_add_fusion
  442.4 4.0 convolution_convert_fusion.3
  447.0 5.0 fusion.62
  453.0 90.5 %while.72 = (s32[]{:T(128)}, f32[128,2,6,128]{3,0,2,1:T(8,128)S(1)}, bf16[128,2,128]{2,0,1:T(8,128)(2,1)S(1)}, bf16[128,2,128]{2,0,1:T(8,128)(2,1)S(1)}, bf16[12...) while((s32[]{:T(128)}, ...), condition=%wide.region_13.14_spmd.clone, body=%wide.region_12.13_spmd.clone.sunk | while | flops 254198032 | bytes 9028110 | solution.py:286
  461.0 3.7 collective-permute-start.5
  470.0 2.2 collective-permute-start.9
  474.2 3.6 collective-permute-start.5
  484.1 3.7 collective-permute-start.5
  493.1 2.2 collective-permute-start.9
  497.3 3.6 collective-permute-start.5
  507.3 3.7 collective-permute-start.5
  516.2 2.3 collective-permute-start.9
  520.4 3.6 collective-permute-start.5
  530.5 3.6 collective-permute-start.5
  539.3 2.2 collective-permute-start.9
  545.6 6.5 fusion.67
  552.2 2.2 copy.90
  554.4 2.5 convert_element_type.175
  557.3 5.2 fusion.57
  562.5 39.2 %all-reduce.3 = (f32[1536]{0:T(1024)S(1)}, f32[2048]{0:T(1024)S(1)}, f32[1536]{0:T(1024)S(1)}) all-reduce(f32[1536]{0:T(1024)S(1)} %get-tuple-element.1022, f32[2048]{0:T(1024)S(1)} %fusion.60, f32[1536]{0:T(1024)S(1)} %copy-done.18), channel_id=4, replica_groups=mesh['shard'=4,'context'=8] {'shard','context'}, use_global_device_ids=true, to_apply=%region_16.17.clone | all-reduce | flops 5120 | bytes 40960
  604.6 2.8 copy.93
  607.4 2.0 convert_element_type.173
  609.4 102.2 %reduce-scatter.17.cloned.1.call-done = f32[48,1536]{1,0:T(8,128)} async-done(((f32[1536,1536]{1,0:T(8,128)}), f32[48,1536]{1,0:T(8,128)}) %reduce-scatter.17.cloned.1.call-update) | async-done | bytes 294928 | tf_op jit(solution)/shard_map/reduce_scatter | solution.py:304
  711.6 160.4 %reduce-scatter.15.cloned.1.call-done = f32[48,2048]{1,0:T(8,128)} async-done(((f32[1536,2048]{1,0:T(8,128)}), f32[48,2048]{1,0:T(8,128)}) %reduce-scatter.15.cloned.1.call-update) | async-done | bytes 393232 | tf_op jit(solution)/shard_map/reduce_scatter | solution.py:302
  (531 shorter events, 123.4 us)
Async XLA Ops:
  7.2 75.4 %all-gather.6.cloned.1.call-start = ((), (), s32[]{:S(2)}) async-start(), calls=%async_computation.6 | async-start | bytes 7864320 | tf_op jit(solution)/shard_map/all_gather | solution.py:163
  8.0 175.8 %all-gather.8.cloned.1.call-start = ((), (), s32[]{:S(2)}) async-start(), calls=%async_computation.7 | async-start | bytes 5898240 | tf_op jit(solution)/shard_map/all_gather | solution.py:164
  8.7 227.7 %all-gather.10.cloned.1.call-start = ((), (), s32[]{:S(2)}) async-start(), calls=%async_computation.8 | async-start | bytes 8601600 | tf_op jit(solution)/shard_map/all_gather | solution.py:218
  9.4 256.6 %all-gather.12.cloned.1.call-start = ((), (), s32[]{:S(2)}) async-start(), calls=%async_computation.9 | async-start | bytes 4300800 | tf_op jit(solution)/shard_map/all_gather | solution.py:219
  10.0 295.7 %all-gather.14.cloned.1.call-start = ((), (), s32[]{:S(2)}) async-start(), calls=%async_computation.11 | async-start | bytes 3538944 | tf_op jit(solution)/shard_map/all_gather | solution.py:223
  10.6 388.1 %reduce-scatter.13.cloned.1.call-start = ((), (), s32[]{:S(2)}) async-start(), calls=%async_computation.12 | async-start | bytes 7077888 | tf_op jit(solution)/shard_map/reduce_scatter | solution.py:240
  88.0 4.8 collective-permute-start
  92.8 5.5 collective-permute-start
  98.3 5.6 collective-permute-start
  103.9 5.6 collective-permute-start
  109.6 5.6 collective-permute-start
  115.2 5.6 collective-permute-start
  120.9 5.6 collective-permute-start
  126.5 5.6 collective-permute-start
  132.8 6.3 collective-permute-start.2
  139.0 6.3 collective-permute-start.2
  145.4 6.3 collective-permute-start.2
  151.7 6.3 collective-permute-start.2
  158.1 6.3 collective-permute-start.2
  164.4 6.3 collective-permute-start.2
  170.8 6.3 collective-permute-start.2
  177.1 6.3 collective-permute-start.2
  189.8 12.7 %collective-permute-start.10 = (bf16[128,1536]{1,0:T(8,128)(2,1)S(1)}, bf16[128,1536]{1,0:T(8,128)(2,1)S(1)}, u32[]{:S(2)}, u32[]{:S(2)}) collective-permute-start(bf16[128,1536]{1,0:T(8,128)(2,1)S(1)} %get-tuple-element.1094), channel_id=1, source_target_pairs={{0,1},{1,2},{2,3},{3,4},{4,5},{5,6},{6,7},{7,0},{8,9},{9,10},{10,1... | collective-permute-start | bytes 1179656 | tf_op jit(solution)/shard_map/ppermute | solution.py:23
  191.2 11.4 %collective-permute-start.11 = (bf16[128,1536]{1,0:T(8,128)(2,1)S(1)}, bf16[128,1536]{1,0:T(8,128)(2,1)S(1)}, u32[]{:S(2)}, u32[]{:S(2)}) collective-permute-start(bf16[128,1536]{1,0:T(8,128)(2,1)S(1)} %get-tuple-element.1094), channel_id=1, source_target_pairs={{0,7},{1,0},{2,1},{3,2},{4,3},{5,4},{6,5},{7,6},{8,15},{9,8},{10,9... | collective-permute-start | bytes 1179656 | tf_op jit(solution)/shard_map/ppermute | solution.py:26
  202.5 12.6 %collective-permute-start.12 = (bf16[128,1536]{1,0:T(8,128)(2,1)S(1)}, bf16[128,1536]{1,0:T(8,128)(2,1)S(1)}, u32[]{:S(2)}, u32[]{:S(2)}) collective-permute-start(bf16[128,1536]{1,0:T(8,128)(2,1)S(1)} %collective-permute-done.10), channel_id=1, source_target_pairs={{0,1},{1,2},{2,3},{3,4},{4,5},{5,6},{6,7},{7,0},{8,9},{9,10},{10,1... | collective-permute-start | bytes 1179656 | tf_op jit(solution)/shard_map/ppermute | solution.py:23
  202.5 12.6 %collective-permute-start.13 = (bf16[128,1536]{1,0:T(8,128)(2,1)S(1)}, bf16[128,1536]{1,0:T(8,128)(2,1)S(1)}, u32[]{:S(2)}, u32[]{:S(2)}) collective-permute-start(bf16[128,1536]{1,0:T(8,128)(2,1)S(1)} %collective-permute-done.11), channel_id=1, source_target_pairs={{0,7},{1,0},{2,1},{3,2},{4,3},{5,4},{6,5},{7,6},{8,15},{9,8},{10,9... | collective-permute-start | bytes 1179656 | tf_op jit(solution)/shard_map/ppermute | solution.py:26
  215.1 11.1 %collective-permute-start.14 = (bf16[128,1536]{1,0:T(8,128)(2,1)S(1)}, bf16[128,1536]{1,0:T(8,128)(2,1)S(1)}, u32[]{:S(2)}, u32[]{:S(2)}) collective-permute-start(bf16[128,1536]{1,0:T(8,128)(2,1)S(1)} %collective-permute-done.12), channel_id=1, source_target_pairs={{0,1},{1,2},{2,3},{3,4},{4,5},{5,6},{6,7},{7,0},{8,9},{9,10},{10,1... | collective-permute-start | bytes 1179656 | tf_op jit(solution)/shard_map/ppermute | solution.py:23
  215.1 12.4 %collective-permute-start.15 = (bf16[128,1536]{1,0:T(8,128)(2,1)S(1)}, bf16[128,1536]{1,0:T(8,128)(2,1)S(1)}, u32[]{:S(2)}, u32[]{:S(2)}) collective-permute-start(bf16[128,1536]{1,0:T(8,128)(2,1)S(1)} %collective-permute-done.13), channel_id=1, source_target_pairs={{0,7},{1,0},{2,1},{3,2},{4,3},{5,4},{6,5},{7,6},{8,15},{9,8},{10,9... | collective-permute-start | bytes 1179656 | tf_op jit(solution)/shard_map/ppermute | solution.py:26
  226.2 9.4 %collective-permute-start.16 = (bf16[128,1536]{1,0:T(8,128)(2,1)S(1)}, bf16[128,1536]{1,0:T(8,128)(2,1)S(1)}, u32[]{:S(2)}, u32[]{:S(2)}) collective-permute-start(bf16[128,1536]{1,0:T(8,128)(2,1)S(1)} %collective-permute-done.14), channel_id=1, source_target_pairs={{0,1},{1,2},{2,3},{3,4},{4,5},{5,6},{6,7},{7,0},{8,9},{9,10},{10,1... | collective-permute-start | bytes 1179656 | tf_op jit(solution)/shard_map/ppermute | solution.py:23
  329.9 109.9 %reduce-scatter.11.cloned.1.call-start = ((), (), s32[]{:S(2)}) async-start(), calls=%async_computation.10 | async-start | bytes 3538944 | tf_op jit(solution)/shard_map/reduce_scatter | solution.py:226
  338.8 213.4 %reduce-scatter.21.cloned.1.call-start = ((), (), s32[]{:S(2)}) async-start(), calls=%async_computation.16 | async-start | bytes 4423680
  352.6 252.0 %reduce-scatter.19.cloned.1.call-start = ((), (), s32[]{:S(2)}) async-start(), calls=%async_computation.15 | async-start | bytes 8847360
  375.2 336.4 %reduce-scatter.17.cloned.1.call-start = ((), (), s32[]{:S(2)}) async-start(), calls=%async_computation.14 | async-start | bytes 9732096 | tf_op jit(solution)/shard_map/reduce_scatter | solution.py:304
  452.0 420.1 %reduce-scatter.15.cloned.1.call-start = ((), (), s32[]{:S(2)}) async-start(), calls=%async_computation.13 | async-start | bytes 12976128 | tf_op jit(solution)/shard_map/reduce_scatter | solution.py:302
  453.0 8.0 collective-permute-start.5
  454.7 6.3 collective-permute-start.6
  456.0 5.0 collective-permute-start.7
  461.0 13.1 %collective-permute-start.5 = (bf16[128,2,128]{2,0,1:T(8,128)(2,1)S(1)}, bf16[128,2,128]{2,0,1:T(8,128)(2,1)S(1)}, u32[]{:S(2)}, u32[]{:S(2)}) collective-permute-start(bf16[128,2,128]{2,0,1:T(8,128)(2,1)S(1)} %copy.143), channel_id=1, source_target_pairs={{1,0},{2,1},{3,2},{4,3},{5,4},{6,5},{7,6},{0,7},{9,8},{10,9},{11,1... | collective-permute-start | bytes 196616 | tf_op jit(solution)/shard_map/while/body/eval_jaxpr/ppermute | solution.py:36
  464.8 9.4 %collective-permute-start.6 = (bf16[128,2,128]{2,0,1:T(8,128)(2,1)S(1)}, bf16[128,2,128]{2,0,1:T(8,128)(2,1)S(1)}, u32[]{:S(2)}, u32[]{:S(2)}) collective-permute-start(bf16[128,2,128]{2,0,1:T(8,128)(2,1)S(1)} %copy.144), channel_id=1, source_target_pairs={{1,0},{2,1},{3,2},{4,3},{5,4},{6,5},{7,6},{0,7},{9,8},{10,9},{11,1... | collective-permute-start | bytes 196616 | tf_op jit(solution)/shard_map/while/body/eval_jaxpr/ppermute | solution.py:36
  466.0 8.1 collective-permute-start.7
  468.4 4.2 collective-permute-start.8
  470.0 4.2 collective-permute-start.9
  474.2 9.9 %collective-permute-start.5 = (bf16[128,2,128]{2,0,1:T(8,128)(2,1)S(1)}, bf16[128,2,128]{2,0,1:T(8,128)(2,1)S(1)}, u32[]{:S(2)}, u32[]{:S(2)}) collective-permute-start(bf16[128,2,128]{2,0,1:T(8,128)(2,1)S(1)} %copy.143), channel_id=1, source_target_pairs={{1,0},{2,1},{3,2},{4,3},{5,4},{6,5},{7,6},{0,7},{9,8},{10,9},{11,1... | collective-permute-start | bytes 196616 | tf_op jit(solution)/shard_map/while/body/eval_jaxpr/ppermute | solution.py:36
  477.8 6.3 collective-permute-start.6
  479.1 5.0 collective-permute-start.7
  484.1 13.1 %collective-permute-start.5 = (bf16[128,2,128]{2,0,1:T(8,128)(2,1)S(1)}, bf16[128,2,128]{2,0,1:T(8,128)(2,1)S(1)}, u32[]{:S(2)}, u32[]{:S(2)}) collective-permute-start(bf16[128,2,128]{2,0,1:T(8,128)(2,1)S(1)} %copy.143), channel_id=1, source_target_pairs={{1,0},{2,1},{3,2},{4,3},{5,4},{6,5},{7,6},{0,7},{9,8},{10,9},{11,1... | collective-permute-start | bytes 196616 | tf_op jit(solution)/shard_map/while/body/eval_jaxpr/ppermute | solution.py:36
  487.9 9.4 %collective-permute-start.6 = (bf16[128,2,128]{2,0,1:T(8,128)(2,1)S(1)}, bf16[128,2,128]{2,0,1:T(8,128)(2,1)S(1)}, u32[]{:S(2)}, u32[]{:S(2)}) collective-permute-start(bf16[128,2,128]{2,0,1:T(8,128)(2,1)S(1)} %copy.144), channel_id=1, source_target_pairs={{1,0},{2,1},{3,2},{4,3},{5,4},{6,5},{7,6},{0,7},{9,8},{10,9},{11,1... | collective-permute-start | bytes 196616 | tf_op jit(solution)/shard_map/while/body/eval_jaxpr/ppermute | solution.py:36
  489.1 8.1 collective-permute-start.7
  491.5 4.2 collective-permute-start.8
  497.3 9.9 %collective-permute-start.5 = (bf16[128,2,128]{2,0,1:T(8,128)(2,1)S(1)}, bf16[128,2,128]{2,0,1:T(8,128)(2,1)S(1)}, u32[]{:S(2)}, u32[]{:S(2)}) collective-permute-start(bf16[128,2,128]{2,0,1:T(8,128)(2,1)S(1)} %copy.143), channel_id=1, source_target_pairs={{1,0},{2,1},{3,2},{4,3},{5,4},{6,5},{7,6},{0,7},{9,8},{10,9},{11,1... | collective-permute-start | bytes 196616 | tf_op jit(solution)/shard_map/while/body/eval_jaxpr/ppermute | solution.py:36
  500.9 6.3 collective-permute-start.6
  502.2 5.0 collective-permute-start.7
  507.3 13.1 %collective-permute-start.5 = (bf16[128,2,128]{2,0,1:T(8,128)(2,1)S(1)}, bf16[128,2,128]{2,0,1:T(8,128)(2,1)S(1)}, u32[]{:S(2)}, u32[]{:S(2)}) collective-permute-start(bf16[128,2,128]{2,0,1:T(8,128)(2,1)S(1)} %copy.143), channel_id=1, source_target_pairs={{1,0},{2,1},{3,2},{4,3},{5,4},{6,5},{7,6},{0,7},{9,8},{10,9},{11,1... | collective-permute-start | bytes 196616 | tf_op jit(solution)/shard_map/while/body/eval_jaxpr/ppermute | solution.py:36
  511.0 9.4 %collective-permute-start.6 = (bf16[128,2,128]{2,0,1:T(8,128)(2,1)S(1)}, bf16[128,2,128]{2,0,1:T(8,128)(2,1)S(1)}, u32[]{:S(2)}, u32[]{:S(2)}) collective-permute-start(bf16[128,2,128]{2,0,1:T(8,128)(2,1)S(1)} %copy.144), channel_id=1, source_target_pairs={{1,0},{2,1},{3,2},{4,3},{5,4},{6,5},{7,6},{0,7},{9,8},{10,9},{11,1... | collective-permute-start | bytes 196616 | tf_op jit(solution)/shard_map/while/body/eval_jaxpr/ppermute | solution.py:36
  512.3 8.1 collective-permute-start.7
  514.7 4.2 collective-permute-start.8
  516.2 4.2 collective-permute-start.9
  520.4 10.0 %collective-permute-start.5 = (bf16[128,2,128]{2,0,1:T(8,128)(2,1)S(1)}, bf16[128,2,128]{2,0,1:T(8,128)(2,1)S(1)}, u32[]{:S(2)}, u32[]{:S(2)}) collective-permute-start(bf16[128,2,128]{2,0,1:T(8,128)(2,1)S(1)} %copy.143), channel_id=1, source_target_pairs={{1,0},{2,1},{3,2},{4,3},{5,4},{6,5},{7,6},{0,7},{9,8},{10,9},{11,1... | collective-permute-start | bytes 196616 | tf_op jit(solution)/shard_map/while/body/eval_jaxpr/ppermute | solution.py:36
  524.1 6.4 collective-permute-start.6
  525.3 5.1 collective-permute-start.7
  530.5 13.0 %collective-permute-start.5 = (bf16[128,2,128]{2,0,1:T(8,128)(2,1)S(1)}, bf16[128,2,128]{2,0,1:T(8,128)(2,1)S(1)}, u32[]{:S(2)}, u32[]{:S(2)}) collective-permute-start(bf16[128,2,128]{2,0,1:T(8,128)(2,1)S(1)} %copy.143), channel_id=1, source_target_pairs={{1,0},{2,1},{3,2},{4,3},{5,4},{6,5},{7,6},{0,7},{9,8},{10,9},{11,1... | collective-permute-start | bytes 196616 | tf_op jit(solution)/shard_map/while/body/eval_jaxpr/ppermute | solution.py:36
  534.1 9.4 %collective-permute-start.6 = (bf16[128,2,128]{2,0,1:T(8,128)(2,1)S(1)}, bf16[128,2,128]{2,0,1:T(8,128)(2,1)S(1)}, u32[]{:S(2)}, u32[]{:S(2)}) collective-permute-start(bf16[128,2,128]{2,0,1:T(8,128)(2,1)S(1)} %copy.144), channel_id=1, source_target_pairs={{1,0},{2,1},{3,2},{4,3},{5,4},{6,5},{7,6},{0,7},{9,8},{10,9},{11,1... | collective-permute-start | bytes 196616 | tf_op jit(solution)/shard_map/while/body/eval_jaxpr/ppermute | solution.py:36
  535.4 8.1 collective-permute-start.7
  537.7 4.2 collective-permute-start.8
  (65 other events, 926.7 us)
Sparse Core Ops, SparseCore 0:
  9.9 72.7 all-gather.5
  84.5 56.9 all-gather.7
  143.3 74.7 all-gather.9
  219.8 46.1 all-gather.11
  267.5 38.1 all-gather.13
  330.0 68.6 reduce-scatter.12
  401.0 38.7 reduce-scatter.10
  442.9 46.4 reduce-scatter.20
  492.5 76.5 reduce-scatter.18
  575.4 136.1 reduce-scatter.16
  718.2 153.7 reduce-scatter.14
